TPU v7x, 256 devices: a whole 4x4x8 slice. The times are simulated.
256 devices in a mesh: row: 32 (over z_hi, y, core), col: 8 (over z_lo, x).
Axes of the slice: x: 4, y: 4, z: 8 (z_hi: 4, z_lo: 2; z = z_hi * 2 + z_lo), core: 2. Of those that a mesh axis runs over, the one named last changes fastest.
Arguments:
- y_prev: float32 [256, 65536], P('row', 'col'), may hold values from 0 to 0.1
- t_block: float32 [256, 256], P('row', 'col'), may hold values from 0.001 to 0.01
- c2_panel: float32 [256, 65536], P('row', 'col'), may hold values from 0 to 1
- c1_panel: float32 [8192, 256], P('row', 'col'), may hold values from 0 to 1
- z_prev: float32 [8192, 65536], P('row', 'col'), may hold values from 0 to 650
- row_const: float32 [8192], P('row'), may hold values from 0 to 4
- col_const: float32 [65536], P('col'), may hold values from 0 to 1
- log_row_mass: float32 [8192], P('row'), may hold values from -1 to 1
- log_col_mass: float32 [65536], P('col'), may hold values from -1 to 1
- col_warm: float32 [65536], P('col'), may hold values from -3 to 3
Outputs:
- y_rows: float32 [256, 65536], P('row', 'col')
- row_pot: float32 [8192], P('row')
- col_pot: float32 [65536], P('col')
All inputs are finite; a program needn't handle non-finite values.
Results may differ from a plain program's by a relative error of at most 0.0003.
Values sent between devices are 32-bit elements; how exact they have to be, the bound alone decides.
A program may use at most 128 MiB of HBM per device.

v0:
```python
import jax
import jax.numpy as jnp
from jax import lax
from jax.experimental import pallas as pl
from jax.experimental.pallas import tpu as pltpu
from jax.sharding import PartitionSpec as P

MESH = pl.DeviceIdType.MESH
F32 = jnp.float32
BF16 = jnp.bfloat16
ROWS, COLS = 32, 8
NZ, NY = 4, 4
GROUP = 8
PANEL = 256
HEIGHT = 256
WIDTH = 8192
LANES = 128
TILES = WIDTH // LANES
DEPTH = PANEL // ROWS
EPSILON = 5.0
LOW = -1e30

ORDER = (
    (0, 0, 0), (3, 0, 0), (1, 0, 0), (0, 0, 1),
    (0, 3, 0), (0, 1, 0), (2, 0, 0), (3, 0, 1), (1, 0, 1),
    (0, 3, 1), (0, 1, 1), (3, 3, 0), (1, 3, 0), (3, 1, 0), (1, 1, 0),
    (2, 0, 1), (0, 2, 0), (0, 2, 1),
    (3, 3, 1), (1, 3, 1), (3, 1, 1), (1, 1, 1),
    (2, 3, 0), (2, 1, 0), (3, 2, 0), (1, 2, 0), (3, 2, 1), (1, 2, 1),
    (2, 3, 1), (2, 1, 1), (2, 2, 0), (2, 2, 1),
)


def entry(index, column):
    found = jnp.int32(0)
    for k, item in enumerate(ORDER):
        if item[column]:
            found = jnp.where(index == k, jnp.int32(item[column]), found)
    return found


def three_left(a):
    high = a.astype(BF16)
    low = (a - high.astype(F32)).astype(BF16)
    return jnp.concatenate([high, low, high], axis=1)


def three_right(b):
    high = b.astype(BF16)
    low = (b - high.astype(F32)).astype(BF16)
    return jnp.concatenate([high, high, low], axis=0)


def kernel(
    yp_hbm, t_hbm, c2_hbm, c1_hbm, zp_hbm, rc_ref, cc_ref, lr_ref, lc_ref, cw_ref,
    y_out, row_out, col_out,
    w, ybuf, c2c, ypc, tg, trow, tfull, c1g, left, gcol, run_m, run_s, bcast,
    sx, rx1, rx2, mloc, lcol, part1, part2, u, c1x, c2x, c3x, d1x, d2x, d3x,
    z_sem, t_sems, c1_sems, tf_sems, a_send, a_recv, y_recv, yp_send, ym_send, zz_send, core_send,
    r_send, r_recv, x_send, x_recv,
):
    r, q = lax.axis_index("row"), lax.axis_index("col")
    zh, yy, core = r // GROUP, (r // 2) % NY, r % 2
    g = r % GROUP

    def row_at(dz, dy, c):
        return ((zh + dz) % NZ * NY + (yy + dy) % NY) * 2 + c

    def remote(src, dst, send, recv, row, col):
        return pltpu.make_async_remote_copy(
            src_ref=src, dst_ref=dst, send_sem=send, recv_sem=recv,
            device_id=(row, col), device_id_type=MESH,
        )

    def drain(ref, sem):
        pltpu.make_async_copy(ref, ref, sem).wait()

    def other_rows(do):
        def one(j, carry):
            do((r + j) % ROWS)
            return carry

        lax.fori_loop(1, ROWS, one, 0)

    def other_cols(do):
        def one(j, carry):
            do((q + j) % COLS)
            return carry

        lax.fori_loop(1, COLS, one, 0)

    pltpu.make_async_copy(zp_hbm, w, z_sem).start()

    barrier = pltpu.get_barrier_semaphore()

    def greet(row, col):
        pl.semaphore_signal(barrier, inc=1, device_id=(row, col), device_id_type=MESH)

    other_cols(lambda col: greet(r, col))
    other_rows(lambda row: greet(row, q))
    pl.semaphore_wait(barrier, ROWS + COLS - 2)

    pltpu.make_async_copy(t_hbm, tg.at[q], t_sems.at[1]).start()
    other_cols(lambda col: remote(t_hbm, tg.at[q], t_sems.at[0], t_sems.at[1], r, col).start())

    def scatter(half):
        def columns(row):
            return pl.ds(pl.multiple_of(row * 2 * LANES + half * LANES, LANES), LANES)

        def send(row):
            for src, dst in ((c2_hbm, c2c), (yp_hbm, ypc)):
                remote(
                    src.at[:, columns(row)], dst.at[half, r], a_send.at[half], a_recv.at[half], row, q
                ).start()

        other_rows(send)
        for src, dst in ((c2_hbm, c2c), (yp_hbm, ypc)):
            pltpu.make_async_copy(src.at[:, columns(r)], dst.at[half, r], a_recv.at[half]).start()

    scatter(0)

    drain(tg, t_sems.at[1])
    trow[...] = jnp.concatenate([tg[k] for k in range(COLS)], axis=1)
    mine = pl.ds(pl.multiple_of(r * DEPTH, DEPTH), DEPTH)
    other_rows(lambda row: remote(trow, tfull.at[r], tf_sems.at[0], tf_sems.at[1], row, q).start())
    pltpu.make_async_copy(trow, tfull.at[r], tf_sems.at[1]).start()

    scatter(1)
    pltpu.make_async_copy(c1_hbm, c1g.at[q], c1_sems.at[1]).start()
    other_cols(lambda col: remote(c1_hbm, c1g.at[q], c1_sems.at[0], c1_sems.at[1], r, col).start())

    gcol[...] = cw_ref[...] * (1.0 / EPSILON)
    run_m[...] = jnp.full_like(run_m, LOW)
    run_s[...] = jnp.zeros_like(run_s)

    drain(tfull, tf_sems.at[1])
    t_three = three_left(tfull[...].reshape(PANEL, PANEL))
    left[...] = t_three

    def own_block(half):
        drain(c2c, a_recv.at[half])
        block = jnp.dot(
            left[...], three_right(c2c[half].reshape(PANEL, LANES)), preferred_element_type=F32
        )
        ybuf[r * 2 + half] = ypc[half].reshape(PANEL, LANES) + block

    def block_at(dz, dy, c, half):
        return row_at(dz, dy, c) * 2 + half

    def pass_on(dz, dy, half):
        b = block_at(dz, dy, core, half)
        here = ybuf.at[b]
        up, down = row_at(0, 1, core), row_at(0, NY - 1, core)
        if dy == 0:
            remote(here, here, yp_send, y_recv.at[b], up, q).start()
            remote(here, here, ym_send, y_recv.at[b], down, q).start()
            if dz == 0 or (dz == NZ - 1 and half == 0):
                remote(here, here, zz_send, y_recv.at[b], row_at(1, 0, core), q).start()
            if dz == 0 or (dz == 1 and half == 1):
                remote(here, here, zz_send, y_recv.at[b], row_at(NZ - 1, 0, core), q).start()
        if dy == NY - 1 and half == 0:
            remote(here, here, yp_send, y_recv.at[b], up, q).start()
        if dy == 1 and half == 1:
            remote(here, here, ym_send, y_recv.at[b], down, q).start()
        remote(here, here, core_send, y_recv.at[b], row_at(0, 0, 1 - core), q).start()

    def take(index):
        dy, dz, half = entry(index, 0), entry(index, 1), entry(index, 2)
        first, second = block_at(dz, dy, core, half), block_at(dz, dy, 1 - core, half)
        pltpu.make_async_copy(ybuf.at[second], ybuf.at[second], y_recv.at[second]).wait()
        for b in (first, second):
            y_out[:, pl.ds(pl.multiple_of(b * LANES, LANES), LANES)] = ybuf[b, mine, :]
        both = jnp.concatenate([ybuf[first], ybuf[second]], axis=1)
        product = jnp.dot(left[...], three_right(both), preferred_element_type=F32)
        scores = []
        for side, b in enumerate((first, second)):
            at = pl.ds(pl.multiple_of(b * LANES, LANES), LANES)
            level = 0.4 * (w[:, at] + product[:, side * LANES : (side + 1) * LANES])
            w[:, at] = level
            scores.append(level + gcol[pl.ds(b, 1), :])
        before = run_m[...]
        peak = jnp.maximum(before, jnp.maximum(scores[0], scores[1]))
        total = run_s[...] * jnp.exp(before - peak)
        run_s[...] = total + jnp.exp(scores[0] - peak) + jnp.exp(scores[1] - peak)
        run_m[...] = peak

    own_block(0)

    def event(index, carry):
        for k, (dy, dz, half) in enumerate(ORDER):

            @pl.when(index == k)
            def _():
                b = block_at(dz, dy, core, half)
                if dy or dz:
                    pltpu.make_async_copy(ybuf.at[b], ybuf.at[b], y_recv.at[b]).wait()
                pass_on(dz, dy, half)

        @pl.when(index == 0)
        def _():
            own_block(1)
            drain(c1g, c1_sems.at[1])
            drain(w, z_sem)
            whole = jnp.concatenate([c1g[k] for k in range(COLS)], axis=1)
            left[...] = three_left(whole)

        @pl.when(index > 0)
        def _():
            take(index - 1)

        return carry

    lax.fori_loop(0, len(ORDER), event, 0)
    take(jnp.int32(len(ORDER) - 1))

    def spread(line):
        return jnp.broadcast_to(line, (LANES, HEIGHT)).T

    def swap_cols(value, slot, buffer):
        sx[slot] = value
        buffer[q] = value
        other_cols(
            lambda col: remote(
                sx.at[slot], buffer.at[q], r_send.at[slot], r_recv.at[slot], r, col
            ).start()
        )
        rest = buffer.at[pl.ds(0, COLS - 1)]
        drain(rest, r_recv.at[slot])
        return buffer[...]

    m_t, s_t = run_m[...].T, run_s[...].T
    peak = jnp.max(m_t, axis=0, keepdims=True)
    line = peak + jnp.log(jnp.sum(s_t * jnp.exp(m_t - peak), axis=0, keepdims=True))
    lines = swap_cols(line, 0, rx1)
    peak = jnp.max(lines, axis=0)
    f1 = lr_ref[...] - peak - jnp.log(jnp.sum(jnp.exp(lines - peak[None]), axis=0))
    bcast[...] = spread(f1)

    def column(b, carry):
        at = pl.ds(pl.multiple_of(b * LANES, LANES), LANES)
        scores = w[:, at] + bcast[...]
        top = jnp.max(scores, axis=0, keepdims=True)
        scaled = jnp.exp(scores - top)
        w[:, at] = scaled
        mloc[pl.ds(b, 1), :] = top
        u[pl.ds(b, 1), :] = jnp.sum(scaled, axis=0, keepdims=True)
        return carry

    lax.fori_loop(0, TILES, column, 0, unroll=2)
    lcol[...] = mloc[...] + jnp.log(u[...])

    def swap_rows(source, slot, first, second, third, join):
        def peer(j):
            return zh * GROUP + (g + j) % GROUP

        def group(do):
            def one(j, carry):
                do(peer(j))
                return carry

            lax.fori_loop(1, GROUP, one, 0)

        first[g] = source[pl.ds(pl.multiple_of(g * 8, 8), 8), :]
        group(
            lambda row: remote(
                source.at[pl.ds(pl.multiple_of((row % GROUP) * 8, 8), 8), :],
                first.at[g], x_send.at[slot, 0], x_recv.at[slot, 0], row, q,
            ).start()
        )
        drain(first.at[pl.ds(0, GROUP - 1)], x_recv.at[slot, 0])
        part = join(first[...])
        part1[slot] = part
        second[zh] = part
        for dz in range(1, NZ):
            remote(
                part1.at[slot], second.at[zh], x_send.at[slot, 1], x_recv.at[slot, 1],
                row_at(dz, 0, core), q,
            ).start()
        drain(second.at[pl.ds(0, NZ - 1)], x_recv.at[slot, 1])
        whole = join(second[...])
        part2[slot] = whole
        third[g] = whole
        group(
            lambda row: remote(
                part2.at[slot], third.at[g], x_send.at[slot, 2], x_recv.at[slot, 2], row, q
            ).start()
        )
        drain(third.at[pl.ds(0, GROUP - 1)], x_recv.at[slot, 2])
        return third[...].reshape(TILES, LANES)

    def joined(parts):
        top = jnp.max(parts, axis=0)
        return top + jnp.log(jnp.sum(jnp.exp(parts - top[None]), axis=0))

    g1 = lc_ref[...] - swap_rows(lcol, 0, c1x, c2x, c3x, joined)
    gcol[...] = g1
    u[...] = jnp.exp(g1 + mloc[...])

    def rows(b, total):
        at = pl.ds(pl.multiple_of(b * LANES, LANES), LANES)
        return total + w[:, at] * u[pl.ds(b, 1), :]

    total = lax.fori_loop(0, TILES, rows, jnp.zeros((HEIGHT, LANES), F32), unroll=2)
    run_s[...] = total
    line = jnp.sum(run_s[...].T, axis=0, keepdims=True)
    lines = swap_cols(line, 1, rx2)
    total = jnp.sum(lines, axis=0)
    f2 = lr_ref[...] + f1 - jnp.log(total)
    row_out[...] = rc_ref[...] + EPSILON * f2
    bcast[...] = spread(jnp.exp(lr_ref[...]) / total)

    def columns(b, carry):
        at = pl.ds(pl.multiple_of(b * LANES, LANES), LANES)
        mloc[pl.ds(b, 1), :] = jnp.sum(w[:, at] * bcast[...], axis=0, keepdims=True)
        return carry

    lax.fori_loop(0, TILES, columns, 0, unroll=2)
    lcol2 = mloc
    lcol2[...] = mloc[...] * u[...]
    total = swap_rows(lcol2, 1, d1x, d2x, d3x, lambda parts: jnp.sum(parts, axis=0))
    col_out[...] = cc_ref[...] + EPSILON * (lc_ref[...] + gcol[...] - jnp.log(total))

    drain(tg.at[pl.ds(0, COLS - 1)], t_sems.at[0])
    drain(c1g.at[pl.ds(0, COLS - 1)], c1_sems.at[0])
    drain(tfull.at[pl.ds(0, ROWS - 1)], tf_sems.at[0])
    for half in range(2):
        drain(c2c.at[:, pl.ds(0, ROWS - 1)], a_send.at[half])
    drain(ybuf.at[pl.ds(0, 12)], yp_send)
    drain(ybuf.at[pl.ds(0, 12)], ym_send)
    drain(ybuf.at[pl.ds(0, 6)], zz_send)
    drain(ybuf.at[pl.ds(0, 32)], core_send)
    for slot in range(2):
        drain(rx1.at[pl.ds(0, COLS - 1)], r_send.at[slot])
        drain(c1x.at[pl.ds(0, GROUP - 1)], x_send.at[slot, 0])
        drain(c2x.at[pl.ds(0, NZ - 1)], x_send.at[slot, 1])
        drain(c3x.at[pl.ds(0, GROUP - 1)], x_send.at[slot, 2])


def body(y_prev, t_block, c2_panel, c1_panel, z_prev, row_const, col_const, log_row_mass, log_col_mass, col_warm):
    tall = lambda a: a.reshape(TILES, LANES)
    flat = lambda a: a.reshape(1, HEIGHT)
    hbm = pl.BlockSpec(memory_space=pl.ANY)
    vmem = pl.BlockSpec(memory_space=pltpu.VMEM)
    dma = pltpu.SemaphoreType.DMA
    y_next, row_pot, col_pot = pl.pallas_call(
        kernel,
        out_shape=(
            jax.ShapeDtypeStruct((DEPTH, WIDTH), F32),
            jax.ShapeDtypeStruct((1, HEIGHT), F32),
            jax.ShapeDtypeStruct((TILES, LANES), F32),
        ),
        in_specs=[hbm] * 5 + [vmem] * 5,
        out_specs=(vmem, vmem, vmem),
        scratch_shapes=[
            pltpu.VMEM((HEIGHT, WIDTH), F32),
            pltpu.VMEM((TILES, PANEL, LANES), F32),
            pltpu.VMEM((2, ROWS, DEPTH, LANES), F32),
            pltpu.VMEM((2, ROWS, DEPTH, LANES), F32),
            pltpu.VMEM((COLS, DEPTH, PANEL // COLS), F32),
            pltpu.VMEM((DEPTH, PANEL), F32),
            pltpu.VMEM((ROWS, DEPTH, PANEL), F32),
            pltpu.VMEM((COLS, HEIGHT, PANEL // COLS), F32),
            pltpu.VMEM((HEIGHT, 3 * PANEL), BF16),
            pltpu.VMEM((TILES, LANES), F32),
            pltpu.VMEM((HEIGHT, LANES), F32),
            pltpu.VMEM((HEIGHT, LANES), F32),
            pltpu.VMEM((HEIGHT, LANES), F32),
            pltpu.VMEM((2, 1, HEIGHT), F32),
            pltpu.VMEM((COLS, 1, HEIGHT), F32),
            pltpu.VMEM((COLS, 1, HEIGHT), F32),
            pltpu.VMEM((TILES, LANES), F32),
            pltpu.VMEM((TILES, LANES), F32),
            pltpu.VMEM((2, 8, LANES), F32),
            pltpu.VMEM((2, 8, LANES), F32),
            pltpu.VMEM((TILES, LANES), F32),
            pltpu.VMEM((GROUP, 8, LANES), F32),
            pltpu.VMEM((NZ, 8, LANES), F32),
            pltpu.VMEM((GROUP, 8, LANES), F32),
            pltpu.VMEM((GROUP, 8, LANES), F32),
            pltpu.VMEM((NZ, 8, LANES), F32),
            pltpu.VMEM((GROUP, 8, LANES), F32),
            dma,
            dma((2,)),
            dma((2,)),
            dma((2,)),
            dma((2,)),
            dma((2,)),
            dma((TILES,)),
            dma,
            dma,
            dma,
            dma,
            dma((2,)),
            dma((2,)),
            dma((2, 3)),
            dma((2, 3)),
        ],
        compiler_params=pltpu.CompilerParams(
            collective_id=0, has_side_effects=True, vmem_limit_bytes=56 * 1024 * 1024
        ),
        name="step",
    )(
        y_prev, t_block, c2_panel, c1_panel, z_prev, flat(row_const), tall(col_const),
        flat(log_row_mass), tall(log_col_mass), tall(col_warm),
    )
    return y_next, row_pot.reshape(HEIGHT), col_pot.reshape(WIDTH)


def solution(mesh):
    block = P("row", "col")
    return jax.shard_map(
        body,
        mesh=mesh,
        in_specs=(block,) * 5 + (P("row"), P("col"), P("row"), P("col"), P("col")),
        out_specs=(block, P("row"), P("col")),
        check_vma=False,
    )
```

profile of v0, /device:TPU:1, one launch (start us, length us, event | category | flops | bytes accessed | tf_op | source)
XLA Modules:
  0.0 136.2 jit_solution(4316432901550775636)
XLA Ops:
  0.6 1.5 %copy.13.c1_hbm = f32[256,32]{1,0:T(8,128)} copy(f32[256,32]{0,1:T(8,128)} %param.13) | data formatting | bytes 65536 | tf_op args[3]
  2.1 129.7 %step.1 = (f32[8,8192]{1,0:T(8,128)}, f32[1,256]{1,0:T(1,128)}, f32[64,128]{1,0:T(8,128)}) custom-call(f32[8,8192]{1,0:T(8,128)} %yp_hbm.1, f32[8,32]{1,0:T(8,128)} %t_hbm.1, f32[8,8192]{1,0:T(8,128)} %c2_hbm.1, f32[256,32]{1,0:T(8,128)} %copy.13.c1_hbm, f32[256,8192]{1,0:T(8,128)} %zp_hbm.1, f32[1,256]{1,0:T(1,128)} %bitcast.11, f32[64,128]{1,0:T(8,128)} %bitcast.7, ...), custom_call_target="tpu_custom_call" | custom-call | tf_op jit(solution)/shard_map/step/pallas_call | solution.py:345
  131.9 1.7 %copy.17 = f32[8,8192]{1,0:T(8,128)} copy(f32[8,8192]{1,0:T(8,128)} %get-tuple-element.12) | data formatting | bytes 524288
  133.6 1.2 copy.18
  134.8 1.4 %copy.19 = f32[8192]{0:T(1024)} copy(f32[8192]{0:T(1024)} %bitcast.10) | data formatting | bytes 65536
where the time goes:
time: 137 us; the launch traced here: 136 us
  Pallas kernels  130 us (95%)
  local copies, waits for them, and re-layouts  5.79 us (4%)
    pallas_call x1, Pallas kernels, body(): pl.pallas_call(kernel, out_shape=(jax.ShapeDtypeStruct((DEPTH, WIDTH), F3...  130 us
    unnamed x4, local copies, waits for them, and re-layouts  5.79 us

commit v1 on v0

--- a/solution.py
+++ b/solution.py
@@ -17,6 +17,7 @@
 LANES = 128
 TILES = WIDTH // LANES
 DEPTH = PANEL // ROWS
+T_COLS = PANEL // COLS
 EPSILON = 5.0
 LOW = -1e30
 
@@ -52,9 +53,9 @@
 
 
 def kernel(
-    yp_hbm, t_hbm, c2_hbm, c1_hbm, zp_hbm, rc_ref, cc_ref, lr_ref, lc_ref, cw_ref,
+    yp_hbm, t_ref, c2_hbm, c1_hbm, zp_hbm, rc_ref, cc_ref, lr_ref, lc_ref, cw_ref,
     y_out, row_out, col_out,
-    w, ybuf, c2c, ypc, tg, trow, tfull, c1g, left, gcol, run_m, run_s, bcast,
+    w, ybuf, c2c, ypc, tpad, tg, trow, tfull, c1g, left, gcol, run_m, run_s, bcast,
     sx, rx1, rx2, mloc, lcol, part1, part2, u, c1x, c2x, c3x, d1x, d2x, d3x,
     z_sem, t_sems, c1_sems, tf_sems, a_send, a_recv, y_recv, yp_send, ym_send, zz_send, core_send,
     r_send, r_recv, x_send, x_recv,
@@ -91,6 +92,8 @@
 
     pltpu.make_async_copy(zp_hbm, w, z_sem).start()
 
+    tpad[...] = jnp.concatenate([t_ref[...]] * (LANES // T_COLS), axis=1)
+
     barrier = pltpu.get_barrier_semaphore()
 
     def greet(row, col):
@@ -100,8 +103,8 @@
     other_rows(lambda row: greet(row, q))
     pl.semaphore_wait(barrier, ROWS + COLS - 2)
 
-    pltpu.make_async_copy(t_hbm, tg.at[q], t_sems.at[1]).start()
-    other_cols(lambda col: remote(t_hbm, tg.at[q], t_sems.at[0], t_sems.at[1], r, col).start())
+    other_cols(lambda col: remote(tpad, tg.at[q], t_sems.at[0], t_sems.at[1], r, col).start())
+    pltpu.make_async_copy(tpad, tg.at[q], t_sems.at[1]).start()
 
     def scatter(half):
         def columns(row):
@@ -120,7 +123,7 @@
     scatter(0)
 
     drain(tg, t_sems.at[1])
-    trow[...] = jnp.concatenate([tg[k] for k in range(COLS)], axis=1)
+    trow[...] = jnp.concatenate([tg[k][:, :T_COLS] for k in range(COLS)], axis=1)
     mine = pl.ds(pl.multiple_of(r * DEPTH, DEPTH), DEPTH)
     other_rows(lambda row: remote(trow, tfull.at[r], tf_sems.at[0], tf_sems.at[1], row, q).start())
     pltpu.make_async_copy(trow, tfull.at[r], tf_sems.at[1]).start()
@@ -201,8 +204,7 @@
             own_block(1)
             drain(c1g, c1_sems.at[1])
             drain(w, z_sem)
-            whole = jnp.concatenate([c1g[k] for k in range(COLS)], axis=1)
-            left[...] = three_left(whole)
+            left[...] = three_left(c1g[...].reshape(PANEL, HEIGHT).T)
 
         @pl.when(index > 0)
         def _():
@@ -336,6 +338,11 @@
         drain(c3x.at[pl.ds(0, GROUP - 1)], x_send.at[slot, 2])
 
 
+def handed_on(*refs):
+    for source, target in zip(refs[:3], refs[3:]):
+        target[...] = source[...]
+
+
 def body(y_prev, t_block, c2_panel, c1_panel, z_prev, row_const, col_const, log_row_mass, log_col_mass, col_warm):
     tall = lambda a: a.reshape(TILES, LANES)
     flat = lambda a: a.reshape(1, HEIGHT)
@@ -349,17 +356,18 @@
             jax.ShapeDtypeStruct((1, HEIGHT), F32),
             jax.ShapeDtypeStruct((TILES, LANES), F32),
         ),
-        in_specs=[hbm] * 5 + [vmem] * 5,
+        in_specs=[hbm, vmem, hbm, hbm, hbm] + [vmem] * 5,
         out_specs=(vmem, vmem, vmem),
         scratch_shapes=[
             pltpu.VMEM((HEIGHT, WIDTH), F32),
             pltpu.VMEM((TILES, PANEL, LANES), F32),
             pltpu.VMEM((2, ROWS, DEPTH, LANES), F32),
             pltpu.VMEM((2, ROWS, DEPTH, LANES), F32),
-            pltpu.VMEM((COLS, DEPTH, PANEL // COLS), F32),
+            pltpu.VMEM((DEPTH, LANES), F32),
+            pltpu.VMEM((COLS, DEPTH, LANES), F32),
             pltpu.VMEM((DEPTH, PANEL), F32),
             pltpu.VMEM((ROWS, DEPTH, PANEL), F32),
-            pltpu.VMEM((COLS, HEIGHT, PANEL // COLS), F32),
+            pltpu.VMEM((COLS, T_COLS, HEIGHT), F32),
             pltpu.VMEM((HEIGHT, 3 * PANEL), BF16),
             pltpu.VMEM((TILES, LANES), F32),
             pltpu.VMEM((HEIGHT, LANES), F32),
@@ -400,9 +408,20 @@
         ),
         name="step",
     )(
-        y_prev, t_block, c2_panel, c1_panel, z_prev, flat(row_const), tall(col_const),
+        y_prev, t_block, c2_panel, c1_panel.T, z_prev, flat(row_const), tall(col_const),
         flat(log_row_mass), tall(log_col_mass), tall(col_warm),
     )
+    y_next, row_pot, col_pot = pl.pallas_call(
+        handed_on,
+        out_shape=(
+            jax.ShapeDtypeStruct((DEPTH, WIDTH), F32),
+            jax.ShapeDtypeStruct((1, HEIGHT), F32),
+            jax.ShapeDtypeStruct((TILES, LANES), F32),
+        ),
+        in_specs=[vmem] * 3,
+        out_specs=(vmem, vmem, vmem),
+        name="results",
+    )(y_next, row_pot, col_pot)
     return y_next, row_pot.reshape(HEIGHT), col_pot.reshape(WIDTH)
 
 

time: 137 us -> 119 us (0.87)
  Pallas kernels: 130 us -> 118 us
  local copies, waits for them, and re-layouts: 5.79 us -> 0 us
    pallas_call x1, Pallas kernels: 130 us -> 116 us  [body(): pl.pallas_call(kernel, out_shape=(jax.ShapeDtypeStruct((DEPTH, WIDTH), F3...]
    unnamed x4 -> x0, local copies, waits for them, and re-layouts: 5.79 us -> none
    pallas_call x0 -> x1, Pallas kernels: none -> 1.68 us  [body(): pl.pallas_call(handed_on, out_shape=(jax.ShapeDtypeStruct((DEPTH, WIDTH),...]
where the time goes in v1:
time: 119 us; the launch traced here: 118 us
  Pallas kernels  118 us (99%)
    pallas_call x1, Pallas kernels, body(): pl.pallas_call(kernel, out_shape=(jax.ShapeDtypeStruct((DEPTH, WIDTH), F3...  116 us

profile of v1, /device:TPU:1, one launch (start us, length us, event | category | flops | bytes accessed | tf_op | source)
XLA Modules:
  0.0 118.4 jit_solution(1632644953866181193)
XLA Ops:
  0.6 116.1 %step.1 = (f32[8,8192]{1,0:T(8,128)}, f32[1,256]{1,0:T(1,128)}, f32[64,128]{1,0:T(8,128)}) custom-call(f32[8,8192]{1,0:T(8,128)} %yp_hbm.1, f32[8,32]{1,0:T(8,128)} %t_ref.1, f32[8,8192]{1,0:T(8,128)} %c2_hbm.1, f32[32,256]{1,0:T(8,128)} %bitcast.8, f32[256,8192]{1,0:T(8,128)} %zp_hbm.1, f32[1,256]{1,0:T(1,128)} %bitcast.12, f32[64,128]{1,0:T(8,128)} %bitcast.9, ...), custom_call_target="tpu_custom_call" | custom-call | tf_op jit(solution)/shard_map/step/pallas_call | solution.py:352
  116.7 1.7 %results.1 = (f32[8,8192]{1,0:T(8,128)}, f32[1,256]{1,0:T(1,128)}, f32[64,128]{1,0:T(8,128)}) custom-call(f32[8,8192]{1,0:T(8,128)} %get-tuple-element.9.refs_0_, f32[1,256]{1,0:T(1,128)} %get-tuple-element.10.refs_1_, f32[64,128]{1,0:T(8,128)} %get-tuple-element.11.refs_2_), custom_call_target="tpu_custom_call" | custom-call | tf_op jit(solution)/shard_map/results/pallas_call | solution.py:414

commit v2 on v1

--- a/solution.py
+++ b/solution.py
@@ -11,6 +11,7 @@
 ROWS, COLS = 32, 8
 NZ, NY = 4, 4
 GROUP = 8
+CHIPS = NZ * NY
 PANEL = 256
 HEIGHT = 256
 WIDTH = 8192
@@ -20,6 +21,7 @@
 T_COLS = PANEL // COLS
 EPSILON = 5.0
 LOW = -1e30
+BEHIND = 1
 
 ORDER = (
     (0, 0, 0), (3, 0, 0), (1, 0, 0), (0, 0, 1),
@@ -32,11 +34,11 @@
 )
 
 
-def entry(index, column):
+def entry(index):
     found = jnp.int32(0)
-    for k, item in enumerate(ORDER):
-        if item[column]:
-            found = jnp.where(index == k, jnp.int32(item[column]), found)
+    for k, (dy, dz, half) in enumerate(ORDER):
+        if k:
+            found = jnp.where(index == k, jnp.int32(dy * 8 + dz * 2 + half), found)
     return found
 
 
@@ -56,9 +58,9 @@
     yp_hbm, t_ref, c2_hbm, c1_hbm, zp_hbm, rc_ref, cc_ref, lr_ref, lc_ref, cw_ref,
     y_out, row_out, col_out,
     w, ybuf, c2c, ypc, tpad, tg, trow, tfull, c1g, left, gcol, run_m, run_s, bcast,
-    sx, rx1, rx2, mloc, lcol, part1, part2, u, c1x, c2x, c3x, d1x, d2x, d3x,
+    sx, rx1, rx2, mloc, lcol, lcol2, part1, part2, u, c1x, c2x, c3x, d1x, d2x, d3x,
     z_sem, t_sems, c1_sems, tf_sems, a_send, a_recv, y_recv, yp_send, ym_send, zz_send, core_send,
-    r_send, r_recv, x_send, x_recv,
+    r_send, r_recv, x_send, x_recv, p_recv, q_recv,
 ):
     r, q = lax.axis_index("row"), lax.axis_index("col")
     zh, yy, core = r // GROUP, (r // 2) % NY, r % 2
@@ -125,8 +127,14 @@
     drain(tg, t_sems.at[1])
     trow[...] = jnp.concatenate([tg[k][:, :T_COLS] for k in range(COLS)], axis=1)
     mine = pl.ds(pl.multiple_of(r * DEPTH, DEPTH), DEPTH)
-    other_rows(lambda row: remote(trow, tfull.at[r], tf_sems.at[0], tf_sems.at[1], row, q).start())
-    pltpu.make_async_copy(trow, tfull.at[r], tf_sems.at[1]).start()
+    pltpu.make_async_copy(trow, tfull.at[r // 2, core], tf_sems.at[1]).start()
+
+    def to_chip(j, carry):
+        row = (r // 2 + j) % CHIPS * 2 + core
+        remote(trow, tfull.at[r // 2, core], tf_sems.at[0], tf_sems.at[1], row, q).start()
+        return carry
+
+    lax.fori_loop(1, CHIPS, to_chip, 0)
 
     scatter(1)
     pltpu.make_async_copy(c1_hbm, c1g.at[q], c1_sems.at[1]).start()
@@ -136,7 +144,10 @@
     run_m[...] = jnp.full_like(run_m, LOW)
     run_s[...] = jnp.zeros_like(run_s)
 
-    drain(tfull, tf_sems.at[1])
+    drain(tfull.at[:, core], tf_sems.at[1])
+    half_t = tfull.at[:, core]
+    remote(half_t, half_t, tf_sems.at[2], tf_sems.at[3], row_at(0, 0, 1 - core), q).start()
+    drain(tfull.at[:, 1 - core], tf_sems.at[3])
     t_three = three_left(tfull[...].reshape(PANEL, PANEL))
     left[...] = t_three
 
@@ -153,22 +164,29 @@
     def pass_on(dz, dy, half):
         b = block_at(dz, dy, core, half)
         here = ybuf.at[b]
-        up, down = row_at(0, 1, core), row_at(0, NY - 1, core)
-        if dy == 0:
-            remote(here, here, yp_send, y_recv.at[b], up, q).start()
-            remote(here, here, ym_send, y_recv.at[b], down, q).start()
-            if dz == 0 or (dz == NZ - 1 and half == 0):
-                remote(here, here, zz_send, y_recv.at[b], row_at(1, 0, core), q).start()
-            if dz == 0 or (dz == 1 and half == 1):
-                remote(here, here, zz_send, y_recv.at[b], row_at(NZ - 1, 0, core), q).start()
-        if dy == NY - 1 and half == 0:
-            remote(here, here, yp_send, y_recv.at[b], up, q).start()
-        if dy == 1 and half == 1:
-            remote(here, here, ym_send, y_recv.at[b], down, q).start()
+        near, first = dy == 0, half == 0
+        start = near & (dz == 0)
+
+        def hand(condition, send, row):
+            @pl.when(condition)
+            def _():
+                remote(here, here, send, y_recv.at[b], row, q).start()
+
+        @pl.when(~start)
+        def _():
+            pltpu.make_async_copy(here, here, y_recv.at[b]).wait()
+
+        hand(near | ((dy == NY - 1) & first), yp_send, row_at(0, 1, core))
+        hand(near | ((dy == 1) & ~first), ym_send, row_at(0, NY - 1, core))
+        hand(start | (near & (dz == NZ - 1) & first), zz_send, row_at(1, 0, core))
+        hand(start | (near & (dz == 1) & ~first), zz_send, row_at(NZ - 1, 0, core))
         remote(here, here, core_send, y_recv.at[b], row_at(0, 0, 1 - core), q).start()
 
-    def take(index):
-        dy, dz, half = entry(index, 0), entry(index, 1), entry(index, 2)
+    def parted(code):
+        return code // 8, code // 2 % 4, code % 2
+
+    def take(code):
+        dy, dz, half = parted(code)
         first, second = block_at(dz, dy, core, half), block_at(dz, dy, 1 - core, half)
         pltpu.make_async_copy(ybuf.at[second], ybuf.at[second], y_recv.at[second]).wait()
         for b in (first, second):
@@ -189,15 +207,13 @@
 
     own_block(0)
 
-    def event(index, carry):
-        for k, (dy, dz, half) in enumerate(ORDER):
-
-            @pl.when(index == k)
-            def _():
-                b = block_at(dz, dy, core, half)
-                if dy or dz:
-                    pltpu.make_async_copy(ybuf.at[b], ybuf.at[b], y_recv.at[b]).wait()
-                pass_on(dz, dy, half)
+    def event(index, before):
+        code = entry(index)
+        dy, dz, half = parted(code)
+
+        @pl.when(index < len(ORDER))
+        def _():
+            pass_on(dz, dy, half)
 
         @pl.when(index == 0)
         def _():
@@ -206,14 +222,13 @@
             drain(w, z_sem)
             left[...] = three_left(c1g[...].reshape(PANEL, HEIGHT).T)
 
-        @pl.when(index > 0)
-        def _():
-            take(index - 1)
-
-        return carry
-
-    lax.fori_loop(0, len(ORDER), event, 0)
-    take(jnp.int32(len(ORDER) - 1))
+        @pl.when(index >= BEHIND)
+        def _():
+            take(before[-1])
+
+        return (code, *before[:-1])
+
+    lax.fori_loop(0, len(ORDER) + BEHIND, event, (jnp.int32(0),) * BEHIND)
 
     def spread(line):
         return jnp.broadcast_to(line, (LANES, HEIGHT)).T
@@ -238,72 +253,95 @@
     f1 = lr_ref[...] - peak - jnp.log(jnp.sum(jnp.exp(lines - peak[None]), axis=0))
     bcast[...] = spread(f1)
 
-    def column(b, carry):
-        at = pl.ds(pl.multiple_of(b * LANES, LANES), LANES)
-        scores = w[:, at] + bcast[...]
-        top = jnp.max(scores, axis=0, keepdims=True)
-        scaled = jnp.exp(scores - top)
-        w[:, at] = scaled
-        mloc[pl.ds(b, 1), :] = top
-        u[pl.ds(b, 1), :] = jnp.sum(scaled, axis=0, keepdims=True)
-        return carry
-
-    lax.fori_loop(0, TILES, column, 0, unroll=2)
-    lcol[...] = mloc[...] + jnp.log(u[...])
-
-    def swap_rows(source, slot, first, second, third, join):
-        def peer(j):
-            return zh * GROUP + (g + j) % GROUP
-
-        def group(do):
-            def one(j, carry):
-                do(peer(j))
-                return carry
-
-            lax.fori_loop(1, GROUP, one, 0)
-
+    def tile(b):
+        return pl.ds(pl.multiple_of(b * LANES, LANES), LANES)
+
+    def part_at(j):
+        pair = j // 2
+        dy = jnp.where(pair == 0, 2, jnp.where(pair == 1, 1, jnp.where(pair == 2, 3, 0)))
+        return (yy + dy) % NY * 2 + (core + 1 + j) % 2
+
+    def column_parts(work, source, slot, first):
+        def one(j, carry):
+            part = part_at(j)
+            at = pl.ds(pl.multiple_of(part * 8, 8), 8)
+            work(part * 8, at)
+
+            @pl.when(j < GROUP - 1)
+            def _():
+                remote(
+                    source.at[at, :], first.at[g], x_send.at[slot, 0], x_recv.at[slot, 0],
+                    zh * GROUP + part, q,
+                ).start()
+
+            return carry
+
+        lax.fori_loop(0, GROUP, one, 0)
+
+    def first_columns(b, at):
+        tops, sums = [], []
+        for k in range(8):
+            scores = w[:, tile(b + k)] + bcast[...]
+            top = jnp.max(scores, axis=0, keepdims=True)
+            scaled = jnp.exp(scores - top)
+            w[:, tile(b + k)] = scaled
+            tops.append(top)
+            sums.append(jnp.sum(scaled, axis=0, keepdims=True))
+        top = jnp.concatenate(tops, axis=0)
+        mloc[at, :] = top
+        lcol[at, :] = top + jnp.log(jnp.concatenate(sums, axis=0))
+
+    column_parts(first_columns, lcol, 0, c1x)
+
+    def join_rows(source, slot, first, second, third, join, p_recv):
         first[g] = source[pl.ds(pl.multiple_of(g * 8, 8), 8), :]
-        group(
-            lambda row: remote(
-                source.at[pl.ds(pl.multiple_of((row % GROUP) * 8, 8), 8), :],
-                first.at[g], x_send.at[slot, 0], x_recv.at[slot, 0], row, q,
-            ).start()
-        )
         drain(first.at[pl.ds(0, GROUP - 1)], x_recv.at[slot, 0])
         part = join(first[...])
         part1[slot] = part
-        second[zh] = part
-        for dz in range(1, NZ):
+        for dz in (2, 1, 3):
             remote(
                 part1.at[slot], second.at[zh], x_send.at[slot, 1], x_recv.at[slot, 1],
                 row_at(dz, 0, core), q,
             ).start()
+        second[zh] = part
         drain(second.at[pl.ds(0, NZ - 1)], x_recv.at[slot, 1])
         whole = join(second[...])
         part2[slot] = whole
+
+        def one(j, carry):
+            row = zh * GROUP + part_at(j)
+            remote(part2.at[slot], third.at[g], x_send.at[slot, 2], p_recv.at[g], row, q).start()
+            return carry
+
+        lax.fori_loop(0, GROUP - 1, one, 0)
         third[g] = whole
-        group(
-            lambda row: remote(
-                part2.at[slot], third.at[g], x_send.at[slot, 2], x_recv.at[slot, 2], row, q
-            ).start()
-        )
-        drain(third.at[pl.ds(0, GROUP - 1)], x_recv.at[slot, 2])
-        return third[...].reshape(TILES, LANES)
 
     def joined(parts):
         top = jnp.max(parts, axis=0)
         return top + jnp.log(jnp.sum(jnp.exp(parts - top[None]), axis=0))
 
-    g1 = lc_ref[...] - swap_rows(lcol, 0, c1x, c2x, c3x, joined)
-    gcol[...] = g1
-    u[...] = jnp.exp(g1 + mloc[...])
-
-    def rows(b, total):
-        at = pl.ds(pl.multiple_of(b * LANES, LANES), LANES)
-        return total + w[:, at] * u[pl.ds(b, 1), :]
-
-    total = lax.fori_loop(0, TILES, rows, jnp.zeros((HEIGHT, LANES), F32), unroll=2)
-    run_s[...] = total
+    join_rows(lcol, 0, c1x, c2x, c3x, joined, p_recv)
+    run_s[...] = jnp.zeros_like(run_s)
+
+    def rows(step, carry):
+        part = part_at(GROUP - 1 - step)
+
+        @pl.when(step > 0)
+        def _():
+            drain(c3x.at[part], p_recv.at[part])
+
+        at = pl.ds(pl.multiple_of(part * 8, 8), 8)
+        level = lc_ref[at, :] - c3x[part]
+        gcol[at, :] = level
+        scale = jnp.exp(level + mloc[at, :])
+        u[at, :] = scale
+        total = run_s[...]
+        for k in range(8):
+            total = total + w[:, tile(part * 8 + k)] * scale[k : k + 1, :]
+        run_s[...] = total
+        return carry
+
+    lax.fori_loop(0, GROUP, rows, 0)
     line = jnp.sum(run_s[...].T, axis=0, keepdims=True)
     lines = swap_cols(line, 1, rx2)
     total = jnp.sum(lines, axis=0)
@@ -311,20 +349,31 @@
     row_out[...] = rc_ref[...] + EPSILON * f2
     bcast[...] = spread(jnp.exp(lr_ref[...]) / total)
 
-    def columns(b, carry):
-        at = pl.ds(pl.multiple_of(b * LANES, LANES), LANES)
-        mloc[pl.ds(b, 1), :] = jnp.sum(w[:, at] * bcast[...], axis=0, keepdims=True)
+    def second_columns(b, at):
+        sums = [jnp.sum(w[:, tile(b + k)] * bcast[...], axis=0, keepdims=True) for k in range(8)]
+        lcol2[at, :] = jnp.concatenate(sums, axis=0) * u[at, :]
+
+    column_parts(second_columns, lcol2, 1, d1x)
+    join_rows(lcol2, 1, d1x, d2x, d3x, lambda parts: jnp.sum(parts, axis=0), q_recv)
+
+    def result(step, carry):
+        part = part_at(GROUP - 1 - step)
+
+        @pl.when(step > 0)
+        def _():
+            drain(d3x.at[part], q_recv.at[part])
+
+        at = pl.ds(pl.multiple_of(part * 8, 8), 8)
+        level = lc_ref[at, :] + gcol[at, :] - jnp.log(d3x[part])
+        col_out[at, :] = cc_ref[at, :] + EPSILON * level
         return carry
 
-    lax.fori_loop(0, TILES, columns, 0, unroll=2)
-    lcol2 = mloc
-    lcol2[...] = mloc[...] * u[...]
-    total = swap_rows(lcol2, 1, d1x, d2x, d3x, lambda parts: jnp.sum(parts, axis=0))
-    col_out[...] = cc_ref[...] + EPSILON * (lc_ref[...] + gcol[...] - jnp.log(total))
+    lax.fori_loop(0, GROUP, result, 0)
 
     drain(tg.at[pl.ds(0, COLS - 1)], t_sems.at[0])
     drain(c1g.at[pl.ds(0, COLS - 1)], c1_sems.at[0])
-    drain(tfull.at[pl.ds(0, ROWS - 1)], tf_sems.at[0])
+    drain(tfull.at[pl.ds(0, CHIPS - 1), 0], tf_sems.at[0])
+    drain(tfull.at[:, 0], tf_sems.at[2])
     for half in range(2):
         drain(c2c.at[:, pl.ds(0, ROWS - 1)], a_send.at[half])
     drain(ybuf.at[pl.ds(0, 12)], yp_send)
@@ -366,7 +415,7 @@
             pltpu.VMEM((DEPTH, LANES), F32),
             pltpu.VMEM((COLS, DEPTH, LANES), F32),
             pltpu.VMEM((DEPTH, PANEL), F32),
-            pltpu.VMEM((ROWS, DEPTH, PANEL), F32),
+            pltpu.VMEM((CHIPS, 2, DEPTH, PANEL), F32),
             pltpu.VMEM((COLS, T_COLS, HEIGHT), F32),
             pltpu.VMEM((HEIGHT, 3 * PANEL), BF16),
             pltpu.VMEM((TILES, LANES), F32),
@@ -376,6 +425,7 @@
             pltpu.VMEM((2, 1, HEIGHT), F32),
             pltpu.VMEM((COLS, 1, HEIGHT), F32),
             pltpu.VMEM((COLS, 1, HEIGHT), F32),
+            pltpu.VMEM((TILES, LANES), F32),
             pltpu.VMEM((TILES, LANES), F32),
             pltpu.VMEM((TILES, LANES), F32),
             pltpu.VMEM((2, 8, LANES), F32),
@@ -390,7 +440,7 @@
             dma,
             dma((2,)),
             dma((2,)),
-            dma((2,)),
+            dma((4,)),
             dma((2,)),
             dma((2,)),
             dma((TILES,)),
@@ -401,7 +451,9 @@
             dma((2,)),
             dma((2,)),
             dma((2, 3)),
-            dma((2, 3)),
+            dma((2, 2)),
+            dma((GROUP,)),
+            dma((GROUP,)),
         ],
         compiler_params=pltpu.CompilerParams(
             collective_id=0, has_side_effects=True, vmem_limit_bytes=56 * 1024 * 1024

time: 119 us -> 111 us (0.933)
  Pallas kernels: 118 us -> 110 us
    pallas_call x1, Pallas kernels: 116 us -> 109 us  [body(): pl.pallas_call(kernel, out_shape=(jax.ShapeDtypeStruct((DEPTH, WIDTH), F3...]
where the time goes in v2:
time: 111 us
  Pallas kernels  110 us (99%)
    pallas_call x1, Pallas kernels, body(): pl.pallas_call(kernel, out_shape=(jax.ShapeDtypeStruct((DEPTH, WIDTH), F3...  109 us

profile of v2, /device:TPU:1, one launch (start us, length us, event | category | flops | bytes accessed | tf_op | source)
XLA Modules:
  0.0 111.1 jit_solution(7284379190816463848)
XLA Ops:
  0.6 108.8 %step.1 = (f32[8,8192]{1,0:T(8,128)}, f32[1,256]{1,0:T(1,128)}, f32[64,128]{1,0:T(8,128)}) custom-call(f32[8,8192]{1,0:T(8,128)} %yp_hbm.1, f32[8,32]{1,0:T(8,128)} %t_ref.1, f32[8,8192]{1,0:T(8,128)} %c2_hbm.1, f32[32,256]{1,0:T(8,128)} %bitcast.8, f32[256,8192]{1,0:T(8,128)} %zp_hbm.1, f32[1,256]{1,0:T(1,128)} %bitcast.12, f32[64,128]{1,0:T(8,128)} %bitcast.9, ...), custom_call_target="tpu_custom_call" | custom-call | tf_op jit(solution)/shard_map/step/pallas_call | solution.py:401
  109.5 1.7 %results.1 = (f32[8,8192]{1,0:T(8,128)}, f32[1,256]{1,0:T(1,128)}, f32[64,128]{1,0:T(8,128)}) custom-call(f32[8,8192]{1,0:T(8,128)} %get-tuple-element.9.refs_0_, f32[1,256]{1,0:T(1,128)} %get-tuple-element.10.refs_1_, f32[64,128]{1,0:T(8,128)} %get-tuple-element.11.refs_2_), custom_call_target="tpu_custom_call" | custom-call | tf_op jit(solution)/shard_map/results/pallas_call | solution.py:466

commit v3 on v2

--- a/solution.py
+++ b/solution.py
@@ -21,6 +21,8 @@
 T_COLS = PANEL // COLS
 EPSILON = 5.0
 LOW = -1e30
+STRIP = 64
+LOG2E = 1.4426950408889634
 BEHIND = 1
 
 ORDER = (
@@ -42,6 +44,10 @@
     return found
 
 
+def log2(a):
+    return jnp.log(a) * LOG2E
+
+
 def three_left(a):
     high = a.astype(BF16)
     low = (a - high.astype(F32)).astype(BF16)
@@ -55,9 +61,10 @@
 
 
 def kernel(
-    yp_hbm, t_ref, c2_hbm, c1_hbm, zp_hbm, rc_ref, cc_ref, lr_ref, lc_ref, cw_ref,
-    y_out, row_out, col_out,
-    w, ybuf, c2c, ypc, tpad, tg, trow, tfull, c1g, left, gcol, run_m, run_s, bcast,
+    yp_hbm, t_hbm, c2_hbm, c1_hbm, zp_hbm, rc_hbm, cc_hbm, lr_hbm, lc_hbm, cw_hbm,
+    y_hbm, row_out, col_out,
+    t_ref, rc_ref, cc_ref, lr_ref, lc_ref, cw_ref, y_out, in_sems, y_sem,
+    w, ybuf, c2c, ypc, tline, tslab, tall, twhole, c1g, left, gcol, run_m, run_s, bcast,
     sx, rx1, rx2, mloc, lcol, lcol2, part1, part2, u, c1x, c2x, c3x, d1x, d2x, d3x,
     z_sem, t_sems, c1_sems, tf_sems, a_send, a_recv, y_recv, yp_send, ym_send, zz_send, core_send,
     r_send, r_recv, x_send, x_recv, p_recv, q_recv,
@@ -92,9 +99,10 @@
 
         lax.fori_loop(1, COLS, one, 0)
 
-    pltpu.make_async_copy(zp_hbm, w, z_sem).start()
-
-    tpad[...] = jnp.concatenate([t_ref[...]] * (LANES // T_COLS), axis=1)
+    small = ((rc_hbm, rc_ref), (cc_hbm, cc_ref), (lr_hbm, lr_ref), (lc_hbm, lc_ref), (cw_hbm, cw_ref))
+    pltpu.make_async_copy(t_hbm, t_ref, in_sems.at[0]).start()
+    for k, (source, target) in enumerate(small):
+        pltpu.make_async_copy(source, target, in_sems.at[k + 1]).start()
 
     barrier = pltpu.get_barrier_semaphore()
 
@@ -103,59 +111,61 @@
 
     other_cols(lambda col: greet(r, col))
     other_rows(lambda row: greet(row, q))
+    pltpu.make_async_copy(zp_hbm, w, z_sem).start()
+    drain(t_ref, in_sems.at[0])
+    tline[...] = jnp.concatenate([t_ref[k : k + 1, :] for k in range(DEPTH)], axis=1)
     pl.semaphore_wait(barrier, ROWS + COLS - 2)
 
-    other_cols(lambda col: remote(tpad, tg.at[q], t_sems.at[0], t_sems.at[1], r, col).start())
-    pltpu.make_async_copy(tpad, tg.at[q], t_sems.at[1]).start()
-
-    def scatter(half):
+    other_rows(lambda row: remote(tline, tslab.at[r], t_sems.at[0], t_sems.at[1], row, q).start())
+    pltpu.make_async_copy(tline, tslab.at[r], t_sems.at[1]).start()
+
+    def scatter(half, which):
         def columns(row):
             return pl.ds(pl.multiple_of(row * 2 * LANES + half * LANES, LANES), LANES)
 
+        k = half * 2 + which
+        src, dst = ((c2_hbm, c2c), (yp_hbm, ypc))[which]
+
         def send(row):
-            for src, dst in ((c2_hbm, c2c), (yp_hbm, ypc)):
-                remote(
-                    src.at[:, columns(row)], dst.at[half, r], a_send.at[half], a_recv.at[half], row, q
-                ).start()
+            remote(src.at[:, columns(row)], dst.at[half, r], a_send.at[k], a_recv.at[k], row, q).start()
 
         other_rows(send)
-        for src, dst in ((c2_hbm, c2c), (yp_hbm, ypc)):
-            pltpu.make_async_copy(src.at[:, columns(r)], dst.at[half, r], a_recv.at[half]).start()
-
-    scatter(0)
-
-    drain(tg, t_sems.at[1])
-    trow[...] = jnp.concatenate([tg[k][:, :T_COLS] for k in range(COLS)], axis=1)
+        pltpu.make_async_copy(src.at[:, columns(r)], dst.at[half, r], a_recv.at[k]).start()
+
+    scatter(0, 0)
+    scatter(0, 1)
+
+    scatter(1, 0)
+    scatter(1, 1)
     mine = pl.ds(pl.multiple_of(r * DEPTH, DEPTH), DEPTH)
-    pltpu.make_async_copy(trow, tfull.at[r // 2, core], tf_sems.at[1]).start()
-
-    def to_chip(j, carry):
-        row = (r // 2 + j) % CHIPS * 2 + core
-        remote(trow, tfull.at[r // 2, core], tf_sems.at[0], tf_sems.at[1], row, q).start()
-        return carry
-
-    lax.fori_loop(1, CHIPS, to_chip, 0)
-
-    scatter(1)
+
+    drain(tslab, t_sems.at[1])
+    other_cols(lambda col: remote(tslab, tall.at[q], tf_sems.at[0], tf_sems.at[1], r, col).start())
+    pltpu.make_async_copy(tslab, tall.at[q], tf_sems.at[1]).start()
     pltpu.make_async_copy(c1_hbm, c1g.at[q], c1_sems.at[1]).start()
     other_cols(lambda col: remote(c1_hbm, c1g.at[q], c1_sems.at[0], c1_sems.at[1], r, col).start())
 
-    gcol[...] = cw_ref[...] * (1.0 / EPSILON)
+    for k, (_, target) in enumerate(small):
+        drain(target, in_sems.at[k + 1])
+    gcol[...] = cw_ref[...] * (LOG2E / EPSILON)
     run_m[...] = jnp.full_like(run_m, LOW)
     run_s[...] = jnp.zeros_like(run_s)
 
-    drain(tfull.at[:, core], tf_sems.at[1])
-    half_t = tfull.at[:, core]
-    remote(half_t, half_t, tf_sems.at[2], tf_sems.at[3], row_at(0, 0, 1 - core), q).start()
-    drain(tfull.at[:, 1 - core], tf_sems.at[3])
-    t_three = three_left(tfull[...].reshape(PANEL, PANEL))
+    drain(tall, tf_sems.at[1])
+    slabs = [tall[k].reshape(ROWS, DEPTH * T_COLS) for k in range(COLS)]
+    for k in range(DEPTH):
+        rows_k = jnp.concatenate([slab[:, k * T_COLS : (k + 1) * T_COLS] for slab in slabs], axis=1)
+        for side in range(PANEL // LANES):
+            twhole[side, pl.ds(k, ROWS, DEPTH), :] = rows_k[:, side * LANES : (side + 1) * LANES]
+    t_three = three_left(jnp.concatenate([twhole[side] for side in range(PANEL // LANES)], axis=1))
     left[...] = t_three
 
     def own_block(half):
-        drain(c2c, a_recv.at[half])
+        drain(c2c.at[half], a_recv.at[half * 2])
         block = jnp.dot(
             left[...], three_right(c2c[half].reshape(PANEL, LANES)), preferred_element_type=F32
         )
+        drain(ypc.at[half], a_recv.at[half * 2 + 1])
         ybuf[r * 2 + half] = ypc[half].reshape(PANEL, LANES) + block
 
     def block_at(dz, dy, c, half):
@@ -196,13 +206,13 @@
         scores = []
         for side, b in enumerate((first, second)):
             at = pl.ds(pl.multiple_of(b * LANES, LANES), LANES)
-            level = 0.4 * (w[:, at] + product[:, side * LANES : (side + 1) * LANES])
+            level = (2.0 / EPSILON * LOG2E) * (w[:, at] + product[:, side * LANES : (side + 1) * LANES])
             w[:, at] = level
             scores.append(level + gcol[pl.ds(b, 1), :])
         before = run_m[...]
         peak = jnp.maximum(before, jnp.maximum(scores[0], scores[1]))
-        total = run_s[...] * jnp.exp(before - peak)
-        run_s[...] = total + jnp.exp(scores[0] - peak) + jnp.exp(scores[1] - peak)
+        total = run_s[...] * jnp.exp2(before - peak)
+        run_s[...] = total + jnp.exp2(scores[0] - peak) + jnp.exp2(scores[1] - peak)
         run_m[...] = peak
 
     own_block(0)
@@ -229,6 +239,8 @@
         return (code, *before[:-1])
 
     lax.fori_loop(0, len(ORDER) + BEHIND, event, (jnp.int32(0),) * BEHIND)
+
+    pltpu.make_async_copy(y_out, y_hbm, y_sem).start()
 
     def spread(line):
         return jnp.broadcast_to(line, (LANES, HEIGHT)).T
@@ -247,10 +259,10 @@
 
     m_t, s_t = run_m[...].T, run_s[...].T
     peak = jnp.max(m_t, axis=0, keepdims=True)
-    line = peak + jnp.log(jnp.sum(s_t * jnp.exp(m_t - peak), axis=0, keepdims=True))
+    line = peak + log2(jnp.sum(s_t * jnp.exp2(m_t - peak), axis=0, keepdims=True))
     lines = swap_cols(line, 0, rx1)
     peak = jnp.max(lines, axis=0)
-    f1 = lr_ref[...] - peak - jnp.log(jnp.sum(jnp.exp(lines - peak[None]), axis=0))
+    f1 = LOG2E * lr_ref[...] - peak - log2(jnp.sum(jnp.exp2(lines - peak[None]), axis=0))
     bcast[...] = spread(f1)
 
     def tile(b):
@@ -278,18 +290,32 @@
 
         lax.fori_loop(0, GROUP, one, 0)
 
+    def over_strips(value, join):
+        joined = [
+            join(value(pl.ds(at, STRIP)).reshape(STRIP // 8, 8, LANES), axis=0)
+            for at in range(0, HEIGHT, STRIP)
+        ]
+        return join(jnp.stack(joined), axis=0)
+
     def first_columns(b, at):
         tops, sums = [], []
         for k in range(8):
-            scores = w[:, tile(b + k)] + bcast[...]
-            top = jnp.max(scores, axis=0, keepdims=True)
-            scaled = jnp.exp(scores - top)
-            w[:, tile(b + k)] = scaled
-            tops.append(top)
-            sums.append(jnp.sum(scaled, axis=0, keepdims=True))
+            cut = tile(b + k)
+            tops.append(
+                jnp.max(over_strips(lambda rows: w[rows, cut] + bcast[rows, :], jnp.max), axis=0, keepdims=True)
+            )
+        for k in range(8):
+            cut = tile(b + k)
+
+            def scaled(rows):
+                value = jnp.exp2(w[rows, cut] + (bcast[rows, :] - tops[k]))
+                w[rows, cut] = value
+                return value
+
+            sums.append(jnp.sum(over_strips(scaled, jnp.sum), axis=0, keepdims=True))
         top = jnp.concatenate(tops, axis=0)
         mloc[at, :] = top
-        lcol[at, :] = top + jnp.log(jnp.concatenate(sums, axis=0))
+        lcol[at, :] = top + log2(jnp.concatenate(sums, axis=0))
 
     column_parts(first_columns, lcol, 0, c1x)
 
@@ -318,7 +344,7 @@
 
     def joined(parts):
         top = jnp.max(parts, axis=0)
-        return top + jnp.log(jnp.sum(jnp.exp(parts - top[None]), axis=0))
+        return top + log2(jnp.sum(jnp.exp2(parts - top[None]), axis=0))
 
     join_rows(lcol, 0, c1x, c2x, c3x, joined, p_recv)
     run_s[...] = jnp.zeros_like(run_s)
@@ -331,26 +357,35 @@
             drain(c3x.at[part], p_recv.at[part])
 
         at = pl.ds(pl.multiple_of(part * 8, 8), 8)
-        level = lc_ref[at, :] - c3x[part]
+        level = LOG2E * lc_ref[at, :] - c3x[part]
         gcol[at, :] = level
-        scale = jnp.exp(level + mloc[at, :])
+        scale = jnp.exp2(level + mloc[at, :])
         u[at, :] = scale
-        total = run_s[...]
-        for k in range(8):
-            total = total + w[:, tile(part * 8 + k)] * scale[k : k + 1, :]
-        run_s[...] = total
+        for top in range(0, HEIGHT, STRIP):
+            strip = pl.ds(top, STRIP)
+            total = run_s[strip, :]
+            for k in range(8):
+                total = total + w[strip, tile(part * 8 + k)] * scale[k : k + 1, :]
+            run_s[strip, :] = total
         return carry
 
     lax.fori_loop(0, GROUP, rows, 0)
     line = jnp.sum(run_s[...].T, axis=0, keepdims=True)
     lines = swap_cols(line, 1, rx2)
     total = jnp.sum(lines, axis=0)
-    f2 = lr_ref[...] + f1 - jnp.log(total)
-    row_out[...] = rc_ref[...] + EPSILON * f2
+    f2 = LOG2E * lr_ref[...] + f1 - log2(total)
+    row_out[...] = rc_ref[...] + EPSILON / LOG2E * f2
     bcast[...] = spread(jnp.exp(lr_ref[...]) / total)
 
     def second_columns(b, at):
-        sums = [jnp.sum(w[:, tile(b + k)] * bcast[...], axis=0, keepdims=True) for k in range(8)]
+        sums = [jnp.zeros((8, LANES), F32)] * 8
+        for top in range(0, HEIGHT, STRIP):
+            strip = pl.ds(top, STRIP)
+            weight = bcast[strip, :]
+            for k in range(8):
+                product = w[strip, tile(b + k)] * weight
+                sums[k] = sums[k] + jnp.sum(product.reshape(STRIP // 8, 8, LANES), axis=0)
+        sums = [jnp.sum(value, axis=0, keepdims=True) for value in sums]
         lcol2[at, :] = jnp.concatenate(sums, axis=0) * u[at, :]
 
     column_parts(second_columns, lcol2, 1, d1x)
@@ -364,18 +399,18 @@
             drain(d3x.at[part], q_recv.at[part])
 
         at = pl.ds(pl.multiple_of(part * 8, 8), 8)
-        level = lc_ref[at, :] + gcol[at, :] - jnp.log(d3x[part])
-        col_out[at, :] = cc_ref[at, :] + EPSILON * level
+        level = LOG2E * lc_ref[at, :] + gcol[at, :] - log2(d3x[part])
+        col_out[at, :] = cc_ref[at, :] + EPSILON / LOG2E * level
         return carry
 
     lax.fori_loop(0, GROUP, result, 0)
 
-    drain(tg.at[pl.ds(0, COLS - 1)], t_sems.at[0])
+    drain(y_out, y_sem)
+    drain(tslab.at[pl.ds(0, ROWS - 1)], t_sems.at[0])
     drain(c1g.at[pl.ds(0, COLS - 1)], c1_sems.at[0])
-    drain(tfull.at[pl.ds(0, CHIPS - 1), 0], tf_sems.at[0])
-    drain(tfull.at[:, 0], tf_sems.at[2])
-    for half in range(2):
-        drain(c2c.at[:, pl.ds(0, ROWS - 1)], a_send.at[half])
+    drain(tall.at[pl.ds(0, COLS - 1)], tf_sems.at[0])
+    for k in range(4):
+        drain(c2c.at[0, pl.ds(0, ROWS - 1)], a_send.at[k])
     drain(ybuf.at[pl.ds(0, 12)], yp_send)
     drain(ybuf.at[pl.ds(0, 12)], ym_send)
     drain(ybuf.at[pl.ds(0, 6)], zz_send)
@@ -405,17 +440,26 @@
             jax.ShapeDtypeStruct((1, HEIGHT), F32),
             jax.ShapeDtypeStruct((TILES, LANES), F32),
         ),
-        in_specs=[hbm, vmem, hbm, hbm, hbm] + [vmem] * 5,
-        out_specs=(vmem, vmem, vmem),
+        in_specs=[hbm] * 10,
+        out_specs=(hbm, vmem, vmem),
         scratch_shapes=[
+            pltpu.VMEM((DEPTH, T_COLS), F32),
+            pltpu.VMEM((1, HEIGHT), F32),
+            pltpu.VMEM((TILES, LANES), F32),
+            pltpu.VMEM((1, HEIGHT), F32),
+            pltpu.VMEM((TILES, LANES), F32),
+            pltpu.VMEM((TILES, LANES), F32),
+            pltpu.VMEM((DEPTH, WIDTH), F32),
+            dma((6,)),
+            dma,
             pltpu.VMEM((HEIGHT, WIDTH), F32),
             pltpu.VMEM((TILES, PANEL, LANES), F32),
             pltpu.VMEM((2, ROWS, DEPTH, LANES), F32),
             pltpu.VMEM((2, ROWS, DEPTH, LANES), F32),
-            pltpu.VMEM((DEPTH, LANES), F32),
-            pltpu.VMEM((COLS, DEPTH, LANES), F32),
-            pltpu.VMEM((DEPTH, PANEL), F32),
-            pltpu.VMEM((CHIPS, 2, DEPTH, PANEL), F32),
+            pltpu.VMEM((1, PANEL), F32),
+            pltpu.VMEM((ROWS, 1, PANEL), F32),
+            pltpu.VMEM((COLS, ROWS, 1, PANEL), F32),
+            pltpu.VMEM((PANEL // LANES, PANEL, LANES), F32),
             pltpu.VMEM((COLS, T_COLS, HEIGHT), F32),
             pltpu.VMEM((HEIGHT, 3 * PANEL), BF16),
             pltpu.VMEM((TILES, LANES), F32),
@@ -440,9 +484,9 @@
             dma,
             dma((2,)),
             dma((2,)),
+            dma((2,)),
             dma((4,)),
-            dma((2,)),
-            dma((2,)),
+            dma((4,)),
             dma((TILES,)),
             dma,
             dma,

time: 111 us -> 110 us (level)
  no operation moved by 1% of the time
where the time goes in v3:
time: 110 us
  Pallas kernels  109 us (99%)
    pallas_call x1, Pallas kernels, body(): pl.pallas_call(kernel, out_shape=(jax.ShapeDtypeStruct((DEPTH, WIDTH), F3...  108 us

profile of v3, /device:TPU:1, one launch (start us, length us, event | category | flops | bytes accessed | tf_op | source)
XLA Modules:
  0.0 110.1 jit_solution(17193120385126574500)
XLA Ops:
  0.6 107.8 %step.1 = (f32[8,8192]{1,0:T(8,128)}, f32[1,256]{1,0:T(1,128)}, f32[64,128]{1,0:T(8,128)}) custom-call(f32[8,8192]{1,0:T(8,128)} %yp_hbm.1, f32[8,32]{1,0:T(8,128)} %t_hbm.1, f32[8,8192]{1,0:T(8,128)} %c2_hbm.1, f32[32,256]{1,0:T(8,128)} %bitcast.8, f32[256,8192]{1,0:T(8,128)} %zp_hbm.1, f32[1,256]{1,0:T(1,128)} %bitcast.12, f32[64,128]{1,0:T(8,128)} %bitcast.9, ...), custom_call_target="tpu_custom_call" | custom-call | tf_op jit(solution)/shard_map/step/pallas_call | solution.py:436
  108.4 1.7 %results.1 = (f32[8,8192]{1,0:T(8,128)}, f32[1,256]{1,0:T(1,128)}, f32[64,128]{1,0:T(8,128)}) custom-call(f32[8,8192]{1,0:T(8,128)} %get-tuple-element.9.refs_0_, f32[1,256]{1,0:T(1,128)} %get-tuple-element.10.refs_1_, f32[64,128]{1,0:T(8,128)} %get-tuple-element.11.refs_2_), custom_call_target="tpu_custom_call" | custom-call | tf_op jit(solution)/shard_map/results/pallas_call | solution.py:510

commit v4 on v3

--- a/solution.py
+++ b/solution.py
@@ -21,7 +21,7 @@
 T_COLS = PANEL // COLS
 EPSILON = 5.0
 LOW = -1e30
-STRIP = 64
+STRIP = 128
 LOG2E = 1.4426950408889634
 BEHIND = 1
 

time: 110 us -> 110 us (level)
  no operation moved by 1% of the time
where the time goes in v4:
time: 110 us
  Pallas kernels  109 us (99%)
    pallas_call x1, Pallas kernels, body(): pl.pallas_call(kernel, out_shape=(jax.ShapeDtypeStruct((DEPTH, WIDTH), F3...  108 us

profile of v4, /device:TPU:1, one launch (start us, length us, event | category | flops | bytes accessed | tf_op | source)
XLA Modules:
  0.0 110.1 jit_solution(9607473646177554728)
XLA Ops:
  0.6 107.8 %step.1 = (f32[8,8192]{1,0:T(8,128)}, f32[1,256]{1,0:T(1,128)}, f32[64,128]{1,0:T(8,128)}) custom-call(f32[8,8192]{1,0:T(8,128)} %yp_hbm.1, f32[8,32]{1,0:T(8,128)} %t_hbm.1, f32[8,8192]{1,0:T(8,128)} %c2_hbm.1, f32[32,256]{1,0:T(8,128)} %bitcast.8, f32[256,8192]{1,0:T(8,128)} %zp_hbm.1, f32[1,256]{1,0:T(1,128)} %bitcast.12, f32[64,128]{1,0:T(8,128)} %bitcast.9, ...), custom_call_target="tpu_custom_call" | custom-call | tf_op jit(solution)/shard_map/step/pallas_call | solution.py:436
  108.4 1.7 %results.1 = (f32[8,8192]{1,0:T(8,128)}, f32[1,256]{1,0:T(1,128)}, f32[64,128]{1,0:T(8,128)}) custom-call(f32[8,8192]{1,0:T(8,128)} %get-tuple-element.9.refs_0_, f32[1,256]{1,0:T(1,128)} %get-tuple-element.10.refs_1_, f32[64,128]{1,0:T(8,128)} %get-tuple-element.11.refs_2_), custom_call_target="tpu_custom_call" | custom-call | tf_op jit(solution)/shard_map/results/pallas_call | solution.py:510
